TPU v7x, 256 devices: a whole 4x4x8 slice. The times are simulated.
256 devices in a mesh: depth: 64 (over z, y_lo, x), tile: 4 (over y_hi, core).
Axes of the slice: x: 4, y: 4 (y_hi: 2, y_lo: 2; y = y_hi * 2 + y_lo), z: 8, core: 2. Of those that a mesh axis runs over, the one named last changes fastest.
Arguments:
- volume: float32 [2, 64, 225, 512], P(None, 'depth', None, 'tile'), may hold values from 0.1 to 5
- kernel: bfloat16 [64, 225, 81, 225], P('depth'), as said below
- measured: float32 [2, 225, 512], P(None, None, 'tile'), may hold values from 0.2 to 5
Outputs:
- updated: float32 [2, 64, 225, 512], P(None, 'depth', None, 'tile')
Inputs may be any that keep to these rules, and one draw needn't show every extreme that they name: `kernel`: kernel weights are nonnegative.
All inputs are finite; a program needn't handle non-finite values.
Results may differ from a plain program's by a relative error of at most 0.0015.
Values may be sent and summed in bfloat16 or wider, within the bound.
A program may use at most 128 MiB of HBM per device.

v0:
```python
import jax
import jax.numpy as jnp
from jax import lax
from jax.sharding import PartitionSpec as P

KSIDE = 9
COLS = 32


def with_halo(cells, sides, width):
    for axis, dim in sides:
        count = lax.axis_size(axis)
        ends = count - 1
        head = lax.slice_in_dim(cells, 0, width, axis=dim)
        tail = lax.slice_in_dim(cells, cells.shape[dim] - width, cells.shape[dim], axis=dim)
        cells = jnp.concatenate(
            [
                lax.ppermute(tail, axis, [(i, (i + 1) % count) for i in range(ends)]),
                cells,
                lax.ppermute(head, axis, [((i + 1) % count, i) for i in range(ends)]),
            ],
            axis=dim,
        )
    return cells


def stacked(flat, sign, axis, cols, cells):
    half = KSIDE // 2
    extended = jnp.pad(flat, ((0, 0), (half, half)))
    column = lax.iota(jnp.int32, cells) % cols
    pieces = []
    for shift_a in range(-half, half + 1):
        for shift_b in range(-half, half + 1):
            start = (half + sign * shift_a) * cols + half + sign * shift_b
            piece = extended[:, start : start + cells]
            moved = column + sign * shift_b
            keep = (moved >= 0) & (moved < cols)
            pieces.append(jnp.where(keep[None, :], piece, jnp.zeros_like(piece)))
    return jnp.stack(pieces, axis=axis)


def local(volume, kernel, measured):
    frames, local_depths, phases, cells = volume.shape
    cols = COLS
    half = KSIDE // 2
    offsets = kernel.shape[2]
    vol16 = volume.astype(jnp.bfloat16)
    rimmed = with_halo(vol16, (("tile", 3),), half * cols)
    partial_value = []
    for frame in range(frames):
        plane = 0
        flat = kernel[plane].reshape(phases, offsets * phases)
        spread = stacked(rimmed[frame, plane], 1, 0, cols, cells).reshape(offsets * phases, cells)
        total = jnp.dot(flat, spread, preferred_element_type=jnp.float32)
        partial_value.append(total)
    partial_value = jnp.stack(partial_value)
    projection = lax.psum(partial_value, "depth")
    ratio = (measured / projection).astype(jnp.bfloat16)
    ratio_rimmed = with_halo(ratio, (("tile", 2),), half * cols)
    spreads = [
        stacked(ratio_rimmed[frame], -1, 1, cols, cells).reshape(phases * offsets, cells)
        for frame in range(frames)
    ]
    plane = 0
    flat = kernel[plane].reshape(phases * offsets, phases)
    norm = jnp.sum(kernel[plane], axis=(0, 1), dtype=jnp.float32)
    backs = []
    for frame in range(frames):
        back = lax.dot_general(
            flat, spreads[frame], (((0,), (0,)), ((), ())), preferred_element_type=jnp.float32
        )
        backs.append(volume[frame, plane] * back / norm[:, None])
    planes = [jnp.stack(backs)]
    return jnp.stack(planes, axis=1)


def solution(mesh):
    in_specs = (P(None, "depth", None, "tile"), P("depth", None, None, None), P(None, None, "tile"))
    out_specs = P(None, "depth", None, "tile")
    return jax.shard_map(local, mesh=mesh, in_specs=in_specs, out_specs=out_specs, check_vma=False)
```

profile of v0, /device:TPU:1, one launch (start us, length us, event | category | flops | bytes accessed | tf_op | source)
XLA Modules:
  0.0 829.7 jit_solution(5707975148380617097)
XLA Ops:
  6.5 1.0 copy.22
  7.5 5.1 collective-permute-start.1
  12.6 3.0 collective-permute-start
  15.7 9.6 %copy.11 = bf16[1,225,81,225]{3,2,1,0:T(8,128)(2,1)} copy(bf16[1,225,81,225]{3,1,2,0:T(8,128)(2,1)} %param.4) | data formatting | bytes 16402500 | tf_op args[1]
  25.4 15.9 %reshape_squeeze.7 = bf16[225,18225]{1,0:T(8,128)(2,1)} reshape(bf16[1,225,81,225]{3,2,1,0:T(8,128)(2,1)} %copy.11) | data formatting | bytes 16402500 | tf_op jit(solution)/shard_map/reshape;squeeze | solution.py:52
  49.3 0.7 constant_dynamic-update-slice_fusion.7
  50.8 0.7 constant_dynamic-update-slice_fusion.5
  52.9 0.7 constant_dynamic-update-slice_fusion.2
  53.6 0.7 constant_dynamic-update-slice_fusion.1
  54.4 0.7 constant_dynamic-update-slice_fusion
  55.1 2.1 copy-done.1
  57.2 6.7 reshape.74
  114.9 6.8 reshape.75
  121.7 7.3 convolution_bitcast_fusion
  129.1 5.8 convolution_bitcast_fusion.1
  135.6 525.4 %all-reduce.6.cloned.1.call-done = f32[2,225,128]{2,1,0:T(8,128)} async-done(((f32[2,225,128]{2,1,0:T(8,128)}), f32[2,225,128]{2,1,0:T(8,128)}) %all-reduce.6.cloned.1.call-update) | async-done | bytes 230416 | tf_op jit(solution)/shard_map/psum | solution.py:57
  661.1 1.0 fusion.6
  662.1 31.6 %collective-permute-start.3 = (bf16[2,225,128]{2,1,0:T(8,128)(2,1)S(1)}, bf16[2,225,128]{2,1,0:T(8,128)(2,1)S(1)}, u32[]{:S(2)}, u32[]{:S(2)}) collective-permute-start(bf16[2,225,128]{2,1,0:T(8,128)(2,1)S(1)} %fusion.6), channel_id=1, source_target_pairs={{1,0},{2,1},{3,2},{5,4},{6,5},{7,6},{9,8},{10,9},{11,10},{13,12},{... | collective-permute-start | bytes 345608 | tf_op jit(solution)/shard_map/ppermute | solution.py:20
  693.6 4.2 collective-permute-start.2
  697.9 6.2 convert_reduce_fusion
  704.1 14.0 %reshape_squeeze.8 = bf16[18225,225]{1,0:T(8,128)(2,1)} reshape(bf16[1,225,81,225]{3,2,1,0:T(8,128)(2,1)} %copy.11) | data formatting | bytes 16402500 | tf_op jit(solution)/shard_map/reshape;squeeze | solution.py:65
  726.2 0.7 constant_dynamic-update-slice_fusion.169
  726.9 0.7 constant_dynamic-update-slice_fusion.168
  729.8 0.7 constant_dynamic-update-slice_fusion.164
  731.3 0.8 constant_dynamic-update-slice_fusion.162
  732.0 2.9 copy.13
  734.9 7.3 reshape.76
  793.1 5.3 copy.16
  798.4 7.4 reshape.77
  805.8 8.8 %fusion.3 = f32[1,225,128]{2,1,0:T(8,128)S(1)} fusion(bf16[18225,128]{1,0:T(8,128)(2,1)} %reshape.76, bf16[18225,225]{1,0:T(8,128)(2,1)} %reshape_squeeze.8, f32[2,1,225,128]{3,2,1,0:T(8,128)S(1)} %copy.9, f32[225]{0:T(256)S(1)} %convert_reduce_fusion), kind=kOutput, calls=%fused_computation.8 | convolution fusion | flops 1049817600 | bytes 13098150 | tf_op jit(solution)/shard_map/dot_general | solution.py:69
  814.6 7.3 fusion.5
  821.9 0.9 copy.17
  (331 shorter events, 123.1 us)
Async XLA Ops:
  6.5 654.5 %all-reduce.6.cloned.1.call-start = ((), (), s32[]{:S(2)}) async-start(), calls=%async_computation | async-start | bytes 475136 | tf_op jit(solution)/shard_map/psum | solution.py:57
  7.5 33.8 %collective-permute-start.1 = (bf16[2,1,225,128]{3,2,1,0:T(8,128)(2,1)S(1)}, bf16[2,1,225,128]{3,2,1,0:T(8,128)(2,1)S(1)}, u32[]{:S(2)}, u32[]{:S(2)}) collective-permute-start(bf16[2,1,225,128]{3,2,1,0:T(8,128)(2,1)S(1)} %copy.22), channel_id=1, source_target_pairs={{1,0},{2,1},{3,2},{5,4},{6,5},{7,6},{9,8},{10,9},{11,10},{13,12},{... | collective-permute-start | bytes 345608 | tf_op jit(solution)/shard_map/ppermute | solution.py:20
  12.6 28.6 %collective-permute-start = (bf16[2,1,225,128]{3,2,1,0:T(8,128)(2,1)S(1)}, bf16[2,1,225,128]{3,2,1,0:T(8,128)(2,1)S(1)}, u32[]{:S(2)}, u32[]{:S(2)}) collective-permute-start(bf16[2,1,225,128]{3,2,1,0:T(8,128)(2,1)S(1)} %copy.22), channel_id=1, source_target_pairs={{0,1},{1,2},{2,3},{4,5},{5,6},{6,7},{8,9},{9,10},{10,11},{12,13},{... | collective-permute-start | bytes 345608 | tf_op jit(solution)/shard_map/ppermute | solution.py:18
  55.1 2.1 copy-start.1
  114.9 14.2 %slice-start = ((s8[4667392]{0:T(1024)(128)(4,1)}), s8[473088]{0:T(1024)(128)(4,1)S(1)}, s32[]{:S(2)}) async-start(s8[4667392]{0:T(1024)(128)(4,1)} %bitcast.1350), calls=%async_computation.1 | async-start | bytes 946176
  121.7 7.3 slice-start.1
  129.1 532.0 %copy-start.3 = (f32[2,225,128]{2,0,1:T(2,128)S(1)}, f32[2,225,128]{2,0,1:T(2,128)}, u32[]{:S(2)}) copy-start(f32[2,225,128]{2,0,1:T(2,128)} %param.5) | copy-start | bytes 691204
  662.1 42.1 %copy-start.2 = (f32[2,1,225,128]{3,1,2,0:T(1,128)S(1)}, f32[2,1,225,128]{3,1,2,0:T(1,128)}, u32[]{:S(2)}) copy-start(f32[2,1,225,128]{3,1,2,0:T(1,128)} %param.3) | copy-start | bytes 691204
  662.1 56.1 %collective-permute-start.3 = (bf16[2,225,128]{2,1,0:T(8,128)(2,1)S(1)}, bf16[2,225,128]{2,1,0:T(8,128)(2,1)S(1)}, u32[]{:S(2)}, u32[]{:S(2)}) collective-permute-start(bf16[2,225,128]{2,1,0:T(8,128)(2,1)S(1)} %fusion.6), channel_id=1, source_target_pairs={{1,0},{2,1},{3,2},{5,4},{6,5},{7,6},{9,8},{10,9},{11,10},{13,12},{... | collective-permute-start | bytes 345608 | tf_op jit(solution)/shard_map/ppermute | solution.py:20
  693.6 24.5 %collective-permute-start.2 = (bf16[2,225,128]{2,1,0:T(8,128)(2,1)S(1)}, bf16[2,225,128]{2,1,0:T(8,128)(2,1)S(1)}, u32[]{:S(2)}, u32[]{:S(2)}) collective-permute-start(bf16[2,225,128]{2,1,0:T(8,128)(2,1)S(1)} %fusion.6), channel_id=1, source_target_pairs={{0,1},{1,2},{2,3},{4,5},{5,6},{6,7},{8,9},{9,10},{10,11},{12,13},{... | collective-permute-start | bytes 345608 | tf_op jit(solution)/shard_map/ppermute | solution.py:18
  805.8 8.8 %copy-start = (bf16[18225,128]{1,0:T(8,128)(2,1)S(1)}, bf16[18225,128]{1,0:T(8,128)(2,1)}, u32[]{:S(2)}) copy-start(bf16[18225,128]{1,0:T(8,128)(2,1)} %reshape.77) | copy-start | bytes 13996804
Sparse Core Ops, SparseCore 0:
  135.8 525.2 all-reduce.5
where the time goes:
time: 831 us; the launch traced here: 830 us
  waiting for transfers between devices  525 us (63%)
  other arithmetic  137 us (16%)
  local copies, waits for them, and re-layouts  80.1 us (10%)
  starting transfers between devices  43.9 us (5%)
  matrix products  29.3 us (4%)
  between operations  14.2 us (2%)
    psum x1, waiting for transfers between devices, local(): projection = lax.psum(partial_value, 'depth')  525 us
    unnamed x303, other arithmetic  126 us
    ppermute x2, starting transfers between devices, with_halo(): lax.ppermute(head, axis, [((i + 1) % count, i) for i in range(ends)])  36.7 us
  transfers between devices with their start and end apart: 5, of which 1 were waited for; matrix products, arithmetic and copies ran while one was open for 6% of the time, Pallas kernels for 0%

commit v1 on v0

v1 whole, which is shorter than its diff:
```python
import functools

import jax
import jax.numpy as jnp
from jax import lax
from jax.experimental import pallas as pl
from jax.experimental.pallas import tpu as pltpu
from jax.sharding import PartitionSpec as P

KSIDE = 9
HALF = 4
COLS = 32
FRAMES = 2
MESH = pl.DeviceIdType.MESH


def step(plane, lines, tiles, vol, ker, meas, out, kbuf, vbuf, mbuf, vx, rx, mt, acc,
         nrm, psend, precv, zsend, zrecv, ksem, lsem, hs, hr, ps, pr, zs, zr, gs, gr):
    phases = ker.shape[2]
    cells = vol.shape[-1]
    rows = FRAMES * cells
    block = rows // plane
    d = lax.axis_index("depth")
    t = lax.axis_index("tile")
    z = d // plane
    k = d % plane
    first = t == 0
    last = t == tiles - 1

    load_vol = pltpu.make_async_copy(vol, vbuf, lsem.at[0])
    load_meas = pltpu.make_async_copy(meas, mbuf, lsem.at[1])
    load_vol.start()
    load_meas.start()

    def load_kernel(b):
        return pltpu.make_async_copy(ker.at[:, b], kbuf.at[b], ksem.at[b])

    for b in range(KSIDE):
        load_kernel(b).start()

    barrier = pltpu.get_barrier_semaphore()
    for j in range(1, plane):
        pl.semaphore_signal(barrier, inc=1, device_id=(z * plane + (k + j) % plane, t), device_id_type=MESH)
    for j in range(1, lines):
        pl.semaphore_signal(barrier, inc=1, device_id=(((z + j) % lines) * plane + k, t), device_id_type=MESH)

    @pl.when(t < tiles - 1)
    def _():
        for j in range(plane):
            pl.semaphore_signal(barrier, inc=1, device_id=(z * plane + (k + j) % plane, t + 1), device_id_type=MESH)

    @pl.when(t > 0)
    def _():
        for j in range(plane):
            pl.semaphore_signal(barrier, inc=1, device_id=(z * plane + (k + j) % plane, t - 1), device_id_type=MESH)

    @pl.when(first)
    def _():
        vx[:, 0:cells, :] = jnp.zeros((FRAMES, cells, phases), jnp.bfloat16)
        rx[:, 0:cells, :] = jnp.zeros((FRAMES, cells, phases), jnp.bfloat16)

    @pl.when(last)
    def _():
        vx[:, 2 * cells:, :] = jnp.zeros((FRAMES, cells, phases), jnp.bfloat16)
        rx[:, 2 * cells:, :] = jnp.zeros((FRAMES, cells, phases), jnp.bfloat16)

    load_vol.wait()
    for f in range(FRAMES):
        vx[f, cells:2 * cells, :] = vbuf[f, :, 0, :].T.astype(jnp.bfloat16)

    sides = jnp.where(t > 0, 1, 0) + jnp.where(t < tiles - 1, 1, 0)
    pl.semaphore_wait(barrier, plane - 1 + lines - 1 + plane * sides)

    own = vx.at[:, pl.ds(cells, cells), :]
    to_next = pltpu.make_async_remote_copy(
        own, vx.at[:, pl.ds(0, cells), :], hs.at[0], hr.at[0], device_id=(d, t + 1), device_id_type=MESH)
    to_prev = pltpu.make_async_remote_copy(
        own, vx.at[:, pl.ds(2 * cells, cells), :], hs.at[1], hr.at[1], device_id=(d, t - 1), device_id_type=MESH)

    @pl.when(t < tiles - 1)
    def _():
        to_next.start()

    @pl.when(t > 0)
    def _():
        to_prev.start()

    load_meas.wait()
    for f in range(FRAMES):
        mt[f * cells:(f + 1) * cells, :] = mbuf[:, f, :].T

    nrm[...] = jnp.zeros_like(nrm)

    @pl.loop(0, KSIDE)
    def _(b):
        load_kernel(b).wait()
        total = jnp.zeros((1, phases), jnp.float32)
        for a in range(KSIDE):
            total += jnp.sum(kbuf[b, a].astype(jnp.float32), axis=0, keepdims=True)
        nrm[0:1, :] += total

    @pl.when(t > 0)
    def _():
        to_next.wait_recv()

    @pl.when(t < tiles - 1)
    def _():
        to_prev.wait_recv()

    column = lax.broadcasted_iota(jnp.int32, (rows, phases), 0) % COLS

    acc[...] = jnp.zeros_like(acc)

    @pl.loop(0, KSIDE)
    def _(b):
        total = jnp.zeros((rows, phases), jnp.float32)
        for a in range(KSIDE):
            lhs = vx[:, COLS * a:COLS * a + cells, :].reshape(rows, phases)
            total += lax.dot_general(lhs, kbuf[b, a], (((1,), (1,)), ((), ())), preferred_element_type=jnp.float32)
        shift = b - HALF
        moved = column + shift
        keep = (moved >= 0) & (moved < COLS)
        acc[...] += jnp.where(keep, pltpu.roll(total, (rows - shift) % rows, 0), 0.0)

    psend[...] = acc[...].astype(jnp.bfloat16)
    sends = []
    for j in range(1, plane):
        peer = (k + j) % plane
        copy = pltpu.make_async_remote_copy(
            psend.at[pl.ds(pl.multiple_of(peer * block, block), block), :], precv.at[j], ps.at[j], pr.at[j],
            device_id=(z * plane + peer, t), device_id_type=MESH)
        copy.start()
        sends.append(copy)
    mine = pl.ds(pl.multiple_of(k * block, block), block)
    part = acc[mine, :]
    for j in range(1, plane):
        sends[j - 1].wait_recv()
        part += precv[j].astype(jnp.float32)

    zsend[...] = part.astype(jnp.bfloat16)
    for j in range(1, lines):
        peer = (z + j) % lines
        copy = pltpu.make_async_remote_copy(
            zsend, zrecv.at[j], zs.at[j], zr.at[j], device_id=(peer * plane + k, t), device_id_type=MESH)
        copy.start()
        sends.append(copy)
    for j in range(1, lines):
        sends[plane - 1 + j - 1].wait_recv()
        part += zrecv[j].astype(jnp.float32)

    ratio = (mt[mine, :] / part).astype(jnp.bfloat16)
    fk = (k * block) // cells
    rk = (k * block) % cells

    def place(base):
        return rx.at[fk, pl.ds(pl.multiple_of(base + rk, block), block), :]

    rx[fk, pl.ds(pl.multiple_of(cells + rk, block), block), :] = ratio

    def gather(side, j):
        return pltpu.make_async_remote_copy(
            place(cells), place((1 - side) * cells), gs.at[side + 1, j], gr.at[side + 1, j],
            device_id=(z * plane + (k + j) % plane, t + side), device_id_type=MESH)

    for j in range(1, plane):
        gather(0, j).start()

    @pl.when(t < tiles - 1)
    def _():
        for j in range(plane):
            gather(1, j).start()

    @pl.when(t > 0)
    def _():
        for j in range(plane):
            gather(-1, j).start()

    for j in range(1, plane):
        gather(0, j).wait_recv()

    @pl.when(t > 0)
    def _():
        for j in range(plane):
            gather(1, j).wait_recv()

    @pl.when(t < tiles - 1)
    def _():
        for j in range(plane):
            gather(-1, j).wait_recv()

    acc[...] = jnp.zeros_like(acc)

    @pl.loop(0, KSIDE)
    def _(b):
        total = jnp.zeros((rows, phases), jnp.float32)
        for a in range(KSIDE):
            low = 2 * cells - COLS * a
            lhs = rx[:, low:low + cells, :].reshape(rows, phases)
            total += jnp.dot(lhs, kbuf[b, a], preferred_element_type=jnp.float32)
        shift = b - HALF
        moved = column - shift
        keep = (moved >= 0) & (moved < COLS)
        acc[...] += jnp.where(keep, pltpu.roll(total, (rows + shift) % rows, 0), 0.0)

    norm = nrm[0:1, :]
    for f in range(FRAMES):
        scaled = acc[f * cells:(f + 1) * cells, :] / norm
        out[f, :, 0, :] = vbuf[f, :, 0, :] * scaled.T

    for copy in sends:
        copy.wait_send()
    for j in range(1, plane):
        gather(0, j).wait_send()

    @pl.when(t < tiles - 1)
    def _():
        to_next.wait_send()
        for j in range(plane):
            gather(1, j).wait_send()

    @pl.when(t > 0)
    def _():
        to_prev.wait_send()
        for j in range(plane):
            gather(-1, j).wait_send()


def local(depths, tiles, volume, kernel, measured):
    frames, _, phases, cells = volume.shape
    plane = 8 if depths % 8 == 0 else 2
    lines = depths // plane
    rows = frames * cells
    block = rows // plane
    vol = volume.transpose(0, 2, 1, 3)
    ker = kernel.transpose(0, 2, 1, 3).reshape(KSIDE, KSIDE, phases, phases)
    meas = measured.transpose(1, 0, 2)
    bf16, f32 = jnp.bfloat16, jnp.float32
    dma = pltpu.SemaphoreType.DMA
    out = pl.pallas_call(
        functools.partial(step, plane, lines, tiles),
        out_shape=jax.ShapeDtypeStruct((frames, phases, 1, cells), f32),
        in_specs=[pl.BlockSpec(memory_space=pl.ANY)] * 3,
        out_specs=pl.BlockSpec(memory_space=pltpu.VMEM),
        scratch_shapes=[
            pltpu.VMEM((KSIDE, KSIDE, phases, phases), bf16),
            pltpu.VMEM((frames, phases, 1, cells), f32),
            pltpu.VMEM((phases, frames, cells), f32),
            pltpu.VMEM((frames, 3 * cells, phases), bf16),
            pltpu.VMEM((frames, 3 * cells, phases), bf16),
            pltpu.VMEM((rows, phases), f32),
            pltpu.VMEM((rows, phases), f32),
            pltpu.VMEM((8, phases), f32),
            pltpu.VMEM((rows, phases), bf16),
            pltpu.VMEM((plane, block, phases), bf16),
            pltpu.VMEM((block, phases), bf16),
            pltpu.VMEM((lines, block, phases), bf16),
            dma((KSIDE,)), dma((2,)), dma((2,)), dma((2,)),
            dma((plane,)), dma((plane,)), dma((lines,)), dma((lines,)),
            dma((3, plane)), dma((3, plane)),
        ],
        compiler_params=pltpu.CompilerParams(
            collective_id=0, has_side_effects=True),
    )(vol, ker, meas)
    return out.transpose(0, 2, 1, 3)


def solution(mesh):
    in_specs = (P(None, "depth", None, "tile"), P("depth", None, None, None), P(None, None, "tile"))
    out_specs = P(None, "depth", None, "tile")
    return jax.shard_map(
        functools.partial(local, mesh.shape["depth"], mesh.shape["tile"]),
        mesh=mesh, in_specs=in_specs, out_specs=out_specs, check_vma=False)
```

time: 831 us -> 46.7 us (0.06)
  waiting for transfers between devices: 525 us -> 0 us
  other arithmetic: 137 us -> 0 us
  local copies, waits for them, and re-layouts: 80.1 us -> 1.64 us
  Pallas kernels: 0 us -> 45 us
  starting transfers between devices: 43.9 us -> 0 us
  matrix products: 29.3 us -> 0 us
  between operations: 14.2 us -> 0.01 us
    psum x1 -> x0, waiting for transfers between devices: 525 us -> none  [local(): projection = lax.psum(partial_value, 'depth')]
    unnamed x303 -> x0, other arithmetic: 126 us -> none
    pallas_call x0 -> x1, Pallas kernels: none -> 45 us  [local(): pl.pallas_call(functools.partial(step, plane, lines, tiles), out_shape=ja...]
    ppermute x4 -> x0, starting transfers between devices: 43.9 us -> none  [the longest x2 36.7 us: with_halo(): lax.ppermute(head, axis, [((i + 1) % count, i) for i in range(ends)])]
    another operation x5 -> x0, local copies, waits for them, and re-layouts: 39 us -> none  [the longest x1 15.9 us: local(): flat = kernel[plane].reshape(phases, offsets * phases)]
    dot_general x4 -> x0, matrix products: 29.3 us -> none  [the longest x2 16.1 us: local(): lax.dot_general(flat, spreads[frame], (((0,), (0,)), ((), ())), preferred...]
    reshape x4 -> x0, local copies, waits for them, and re-layouts: 28.3 us -> none  [the longest x2 14.7 us: local(): stacked(ratio_rimmed[frame], -1, 1, cols, cells)]
    unnamed x15 -> x1, local copies, waits for them, and re-layouts: 12.8 us -> 1.64 us
  transfers between devices with their start and end apart: 5 -> 0, of which waited for: 1 -> 0; matrix products, arithmetic and copies ran while one was open for 6% -> 0% of each run, Pallas kernels for 0% -> 0%
where the time goes in v1:
time: 46.7 us; the launch traced here: 46.6 us
  Pallas kernels  45 us (96%)
  local copies, waits for them, and re-layouts  1.64 us (4%)
    pallas_call x1, Pallas kernels, local(): pl.pallas_call(functools.partial(step, plane, lines, tiles), out_shape=ja...  45 us
    unnamed x1, local copies, waits for them, and re-layouts  1.64 us

profile of v1, /device:TPU:1, one launch (start us, length us, event | category | flops | bytes accessed | tf_op | source)
XLA Modules:
  0.0 46.6 jit_solution(11232252454386509327)
XLA Ops:
  0.0 45.0 %shard_map.37 = f32[2,225,1,128]{3,2,1,0:T(1,128)} custom-call(f32[2,225,1,128]{3,2,1,0:T(1,128)} %bitcast.8, bf16[9,9,225,225]{3,2,1,0:T(8,128)(2,1)} %bitcast.6, f32[225,2,128]{2,1,0:T(2,128)} %bitcast.9), custom_call_target="tpu_custom_call" | custom-call | tf_op jit(solution)/shard_map/pallas_call | solution.py:239
  45.0 1.6 %copy.5 = f32[2,1,225,128]{3,1,2,0:T(1,128)} copy(f32[2,1,225,128]{3,1,2,0:T(1,128)} %bitcast.7) | data formatting | bytes 460800

commit v2 on v1

v2 whole, which is shorter than its diff:
```python
import functools

import jax
import jax.numpy as jnp
from jax import lax
from jax.experimental import pallas as pl
from jax.experimental.pallas import tpu as pltpu
from jax.sharding import PartitionSpec as P

KSIDE = 9
HALF = 4
COLS = 32
FRAMES = 2
MESH = pl.DeviceIdType.MESH


def partial_sums(src, taps, sign, cells, own, transposed):
    height = cells // COLS
    phases = src.shape[-1]
    sums = [None] * height
    for a in range(KSIDE):
        u = sign * (a - HALF)
        if own:
            low, high = max(0, -u), min(height, height - u)
        else:
            low, high = (max(0, height - u), height) if u > 0 else (0, min(height, -u))
        if low >= high:
            continue
        start = cells + COLS * (low + u)
        count = high - low
        lhs = src[:, start:start + COLS * count, :].reshape(FRAMES * COLS * count, phases)
        dims = (((1,), (1 if transposed else 0,)), ((), ()))
        out = lax.dot_general(lhs, taps[a], dims, preferred_element_type=jnp.float32)
        out = out.reshape(FRAMES, count, COLS, phases)
        for i in range(count):
            piece = out[:, i]
            sums[low + i] = piece if sums[low + i] is None else sums[low + i] + piece
    return jnp.stack(sums, axis=1).reshape(FRAMES * cells, phases)


def step(plane, lines, tiles, vol, ker, meas, out, kbuf, vbuf, mbuf, vx, rx, mt, acc, parts,
         nrm, psend, precv, zsend, zrecv, ksem, lsem, hs, hr, ps, pr, zs, zr, gs, gr, round_sem):
    phases = ker.shape[2]
    cells = vol.shape[-1]
    rows = FRAMES * cells
    block = rows // plane
    d = lax.axis_index("depth")
    t = lax.axis_index("tile")
    z = d // plane
    k = d % plane
    first = t == 0
    last = t == tiles - 1

    load_vol = pltpu.make_async_copy(vol, vbuf, lsem.at[0])
    load_meas = pltpu.make_async_copy(meas, mbuf, lsem.at[1])
    load_vol.start()

    def load_kernel(b):
        return pltpu.make_async_copy(ker.at[:, b], kbuf.at[b], ksem.at[b])

    pair = 1 - 2 * (t % 2)
    far = t - pair
    crossing = (far >= 0) & (far < tiles)
    relayed = plane == 8 and lines == 8

    def tell(sem, depth, tile):
        pl.semaphore_signal(sem, inc=1, device_id=(depth, tile), device_id_type=MESH)

    def along(j):
        return ((z + lines + j) % lines) * plane + k

    def flat(j):
        return z * plane + (k + j) % plane

    across = z * plane + (k + plane // 2) % plane
    barrier = pltpu.get_barrier_semaphore()
    if relayed:
        row = z * plane + (k // 4) * 4
        for j in range(1, 4):
            tell(barrier, row + (k + j) % 4, t)
        tell(barrier, across, t)
        for j in (-2, -1, 1, 2):
            tell(barrier, along(j), t)
        near = 8
    else:
        for j in range(1, plane):
            tell(barrier, flat(j), t)
        for j in range(1, lines):
            tell(barrier, along(j), t)
        near = plane + lines - 2
    tell(barrier, d, t + pair)

    @pl.when(crossing)
    def _():
        tell(barrier, d, far)

    @pl.when(first)
    def _():
        vx[:, 0:cells, :] = jnp.zeros((FRAMES, cells, phases), jnp.bfloat16)
        rx[:, 0:cells, :] = jnp.zeros((FRAMES, cells, phases), jnp.bfloat16)

    @pl.when(last)
    def _():
        vx[:, 2 * cells:, :] = jnp.zeros((FRAMES, cells, phases), jnp.bfloat16)
        rx[:, 2 * cells:, :] = jnp.zeros((FRAMES, cells, phases), jnp.bfloat16)

    load_vol.wait()
    for b in range(KSIDE):
        load_kernel(b).start()
    load_meas.start()
    for f in range(FRAMES):
        vx[f, cells:2 * cells, :] = vbuf[f, :, 0, :].T.astype(jnp.bfloat16)

    pl.semaphore_wait(barrier, near + 1 + jnp.where(crossing, 1, 0))

    own = vx.at[:, pl.ds(cells, cells), :]
    to_next = pltpu.make_async_remote_copy(
        own, vx.at[:, pl.ds(0, cells), :], hs.at[0], hr.at[0], device_id=(d, t + 1), device_id_type=MESH)
    to_prev = pltpu.make_async_remote_copy(
        own, vx.at[:, pl.ds(2 * cells, cells), :], hs.at[1], hr.at[1], device_id=(d, t - 1), device_id_type=MESH)

    @pl.when(t < tiles - 1)
    def _():
        to_next.start()

    @pl.when(t > 0)
    def _():
        to_prev.start()

    if relayed:
        tell(round_sem.at[0], along(-2), t)
        tell(round_sem.at[1], along(2), t)
        tell(round_sem.at[2], across, t)

    load_meas.wait()
    for f in range(FRAMES):
        mt[f * cells:(f + 1) * cells, :] = mbuf[:, f, :].T

    @pl.loop(0, KSIDE)
    def _(b):
        load_kernel(b).wait()
        parts[b] = partial_sums(vx, kbuf.at[b], 1, cells, True, True)

    if relayed:
        pl.semaphore_wait(round_sem.at[2], 1)
    @pl.when(crossing)
    def _():
        tell(round_sem.at[3], d, far)

    @pl.when(t > 0)
    def _():
        to_next.wait_recv()

    @pl.when(t < tiles - 1)
    def _():
        to_prev.wait_recv()

    column = lax.broadcasted_iota(jnp.int32, (rows, phases), 0) % COLS

    def shifted(total, shift):
        if shift == 0:
            return total
        moved = column - shift
        return jnp.where((moved >= 0) & (moved < COLS), pltpu.roll(total, shift % rows, 0), 0.0)

    for b in range(KSIDE):
        total = parts[b] + partial_sums(vx, kbuf.at[b], 1, cells, False, True)
        add = shifted(total, HALF - b)
        acc[...] = add if b == 0 else acc[...] + add

    if relayed:
        pl.semaphore_wait(round_sem.at[0], 1)
        pl.semaphore_wait(round_sem.at[1], 1)

    @pl.when(crossing)
    def _():
        pl.semaphore_wait(round_sem.at[3], 1)

    psend[...] = acc[...].astype(jnp.bfloat16)
    sends = []
    for j in range(1, plane):
        peer = (k + j) % plane
        copy = pltpu.make_async_remote_copy(
            psend.at[pl.ds(pl.multiple_of(peer * block, block), block), :], precv.at[j], ps.at[j], pr.at[j],
            device_id=(z * plane + peer, t), device_id_type=MESH)
        copy.start()
        sends.append(copy)
    nrm[...] = jnp.zeros_like(nrm)

    @pl.loop(0, KSIDE)
    def _(b):
        total = jnp.zeros((1, phases), jnp.float32)
        for a in range(KSIDE):
            total += jnp.sum(kbuf[b, a].astype(jnp.float32), axis=0, keepdims=True)
        nrm[0:1, :] += total

    mine = pl.ds(pl.multiple_of(k * block, block), block)
    part = acc[mine, :]
    for j in range(1, plane):
        sends[j - 1].wait_recv()
        part += precv[j].astype(jnp.float32)

    zsend[...] = part.astype(jnp.bfloat16)
    for j in range(1, lines):
        peer = (z + j) % lines
        copy = pltpu.make_async_remote_copy(
            zsend, zrecv.at[j], zs.at[j], zr.at[j], device_id=(peer * plane + k, t), device_id_type=MESH)
        copy.start()
        sends.append(copy)
    for j in range(1, lines):
        sends[plane - 1 + j - 1].wait_recv()
        part += zrecv[j].astype(jnp.float32)

    ratio = (mt[mine, :] / part).astype(jnp.bfloat16)
    fk = (k * block) // cells
    rk = (k * block) % cells

    def place(base, who):
        f = (who * block) // cells
        r = (who * block) % cells
        return rx.at[f, pl.ds(pl.multiple_of(base + r, block), block), :]

    rx[fk, pl.ds(pl.multiple_of(cells + rk, block), block), :] = ratio

    def gather(j):
        return pltpu.make_async_remote_copy(
            place(cells, k), place(cells, k), gs.at[0, j], gr.at[0, j],
            device_id=(z * plane + (k + j) % plane, t), device_id_type=MESH)

    def cross(j):
        return pltpu.make_async_remote_copy(
            place(cells, k), place((1 + pair) * cells, k), gs.at[1, j], gr.at[1, j],
            device_id=(z * plane + (k + j) % plane, far), device_id_type=MESH)

    def relay(j):
        who = (k + plane - j) % plane
        return pltpu.make_async_remote_copy(
            place(cells, who), place((1 - pair) * cells, who), gs.at[2, j], gr.at[2, j],
            device_id=(d, t + pair), device_id_type=MESH)

    for j in range(1, plane):
        gather(j).start()

    @pl.when(crossing)
    def _():
        for j in range(plane):
            cross(j).start()

    relay(0).start()
    for j in range(1, plane):
        gather(j).wait_recv()
        relay(j).start()

    @pl.loop(0, KSIDE)
    def _(b):
        parts[b] = partial_sums(rx, kbuf.at[b], -1, cells, True, False)

    for j in range(plane):
        relay(j).wait_recv()

    @pl.when(crossing)
    def _():
        for j in range(plane):
            cross(j).wait_recv()

    for b in range(KSIDE):
        total = parts[b] + partial_sums(rx, kbuf.at[b], -1, cells, False, False)
        add = shifted(total, b - HALF)
        acc[...] = add if b == 0 else acc[...] + add

    norm = nrm[0:1, :]
    for f in range(FRAMES):
        scaled = acc[f * cells:(f + 1) * cells, :] / norm
        out[f, :, 0, :] = vbuf[f, :, 0, :] * scaled.T

    for copy in sends:
        copy.wait_send()
    for j in range(1, plane):
        gather(j).wait_send()
    for j in range(plane):
        relay(j).wait_send()

    @pl.when(crossing)
    def _():
        for j in range(plane):
            cross(j).wait_send()

    @pl.when(t < tiles - 1)
    def _():
        to_next.wait_send()

    @pl.when(t > 0)
    def _():
        to_prev.wait_send()


def local(depths, tiles, volume, kernel, measured):
    frames, _, phases, cells = volume.shape
    plane = 8 if depths % 8 == 0 else 2
    lines = depths // plane
    rows = frames * cells
    block = rows // plane
    vol = volume.transpose(0, 2, 1, 3)
    ker = kernel.transpose(0, 2, 1, 3).reshape(KSIDE, KSIDE, phases, phases)
    meas = measured.transpose(1, 0, 2)
    bf16, f32 = jnp.bfloat16, jnp.float32
    dma = pltpu.SemaphoreType.DMA
    out = pl.pallas_call(
        functools.partial(step, plane, lines, tiles),
        out_shape=jax.ShapeDtypeStruct((frames, phases, 1, cells), f32),
        in_specs=[pl.BlockSpec(memory_space=pl.ANY)] * 3,
        out_specs=pl.BlockSpec(memory_space=pltpu.VMEM),
        scratch_shapes=[
            pltpu.VMEM((KSIDE, KSIDE, phases, phases), bf16),
            pltpu.VMEM((frames, phases, 1, cells), f32),
            pltpu.VMEM((phases, frames, cells), f32),
            pltpu.VMEM((frames, 3 * cells, phases), bf16),
            pltpu.VMEM((frames, 3 * cells, phases), bf16),
            pltpu.VMEM((rows, phases), f32),
            pltpu.VMEM((rows, phases), f32),
            pltpu.VMEM((KSIDE, rows, phases), f32),
            pltpu.VMEM((8, phases), f32),
            pltpu.VMEM((rows, phases), bf16),
            pltpu.VMEM((plane, block, phases), bf16),
            pltpu.VMEM((block, phases), bf16),
            pltpu.VMEM((lines, block, phases), bf16),
            dma((KSIDE,)), dma((2,)), dma((2,)), dma((2,)),
            dma((plane,)), dma((plane,)), dma((lines,)), dma((lines,)),
            dma((3, plane)), dma((3, plane)),
            pltpu.SemaphoreType.REGULAR((4,)),
        ],
        compiler_params=pltpu.CompilerParams(
            collective_id=0, has_side_effects=True),
    )(vol, ker, meas)
    return out.transpose(0, 2, 1, 3)


def solution(mesh):
    in_specs = (P(None, "depth", None, "tile"), P("depth", None, None, None), P(None, None, "tile"))
    out_specs = P(None, "depth", None, "tile")
    return jax.shard_map(
        functools.partial(local, mesh.shape["depth"], mesh.shape["tile"]),
        mesh=mesh, in_specs=in_specs, out_specs=out_specs, check_vma=False)
```

time: 46.7 us -> 40.6 us (0.87)
  Pallas kernels: 45 us -> 38.8 us
    pallas_call x1, Pallas kernels: 45 us -> 38.8 us  [local(): pl.pallas_call(functools.partial(step, plane, lines, tiles), out_shape=ja...]
where the time goes in v2:
time: 40.6 us; the launch traced here: 40.5 us
  Pallas kernels  38.8 us (96%)
  local copies, waits for them, and re-layouts  1.64 us (4%)
    pallas_call x1, Pallas kernels, local(): pl.pallas_call(functools.partial(step, plane, lines, tiles), out_shape=ja...  38.8 us
    unnamed x1, local copies, waits for them, and re-layouts  1.64 us

profile of v2, /device:TPU:1, one launch (start us, length us, event | category | flops | bytes accessed | tf_op | source)
XLA Modules:
  0.0 40.5 jit_solution(803096203543883765)
XLA Ops:
  0.0 38.8 %shard_map.37 = f32[2,225,1,128]{3,2,1,0:T(1,128)} custom-call(f32[2,225,1,128]{3,2,1,0:T(1,128)} %bitcast.8, bf16[9,9,225,225]{3,2,1,0:T(8,128)(2,1)} %bitcast.6, f32[225,2,128]{2,1,0:T(2,128)} %bitcast.9), custom_call_target="tpu_custom_call" | custom-call | tf_op jit(solution)/shard_map/pallas_call | solution.py:308
  38.8 1.6 %copy.5 = f32[2,1,225,128]{3,1,2,0:T(1,128)} copy(f32[2,1,225,128]{3,1,2,0:T(1,128)} %bitcast.7) | data formatting | bytes 460800

commit v3 on v2

--- a/solution.py
+++ b/solution.py
@@ -177,38 +177,28 @@
         pl.semaphore_wait(round_sem.at[3], 1)
 
     psend[...] = acc[...].astype(jnp.bfloat16)
-    sends = []
     for j in range(1, plane):
         peer = (k + j) % plane
-        copy = pltpu.make_async_remote_copy(
-            psend.at[pl.ds(pl.multiple_of(peer * block, block), block), :], precv.at[j], ps.at[j], pr.at[j],
-            device_id=(z * plane + peer, t), device_id_type=MESH)
-        copy.start()
-        sends.append(copy)
-    nrm[...] = jnp.zeros_like(nrm)
-
-    @pl.loop(0, KSIDE)
-    def _(b):
-        total = jnp.zeros((1, phases), jnp.float32)
-        for a in range(KSIDE):
-            total += jnp.sum(kbuf[b, a].astype(jnp.float32), axis=0, keepdims=True)
-        nrm[0:1, :] += total
-
+        pltpu.make_async_remote_copy(
+            psend.at[pl.ds(pl.multiple_of(peer * block, block), block), :], precv.at[j], ps, pr,
+            device_id=(z * plane + peer, t), device_id_type=MESH).start()
+
+    def landed(ref, sem):
+        pltpu.make_async_copy(ref, ref, sem).wait()
+
+    others = pl.ds(1, plane - 1)
     mine = pl.ds(pl.multiple_of(k * block, block), block)
     part = acc[mine, :]
+    landed(precv.at[others], pr)
     for j in range(1, plane):
-        sends[j - 1].wait_recv()
         part += precv[j].astype(jnp.float32)
 
     zsend[...] = part.astype(jnp.bfloat16)
     for j in range(1, lines):
-        peer = (z + j) % lines
-        copy = pltpu.make_async_remote_copy(
-            zsend, zrecv.at[j], zs.at[j], zr.at[j], device_id=(peer * plane + k, t), device_id_type=MESH)
-        copy.start()
-        sends.append(copy)
+        pltpu.make_async_remote_copy(
+            zsend, zrecv.at[j], zs, zr, device_id=(along(j), t), device_id_type=MESH).start()
+    landed(zrecv.at[pl.ds(1, lines - 1)], zr)
     for j in range(1, lines):
-        sends[plane - 1 + j - 1].wait_recv()
         part += zrecv[j].astype(jnp.float32)
 
     ratio = (mt[mine, :] / part).astype(jnp.bfloat16)
@@ -222,46 +212,44 @@
 
     rx[fk, pl.ds(pl.multiple_of(cells + rk, block), block), :] = ratio
 
-    def gather(j):
-        return pltpu.make_async_remote_copy(
-            place(cells, k), place(cells, k), gs.at[0, j], gr.at[0, j],
-            device_id=(z * plane + (k + j) % plane, t), device_id_type=MESH)
-
-    def cross(j):
-        return pltpu.make_async_remote_copy(
-            place(cells, k), place((1 + pair) * cells, k), gs.at[1, j], gr.at[1, j],
-            device_id=(z * plane + (k + j) % plane, far), device_id_type=MESH)
-
-    def relay(j):
-        who = (k + plane - j) % plane
-        return pltpu.make_async_remote_copy(
-            place(cells, who), place((1 - pair) * cells, who), gs.at[2, j], gr.at[2, j],
-            device_id=(d, t + pair), device_id_type=MESH)
-
     for j in range(1, plane):
-        gather(j).start()
+        pltpu.make_async_remote_copy(
+            place(cells, k), place(cells, k), gs.at[0], gr.at[0],
+            device_id=(flat(j), t), device_id_type=MESH).start()
 
     @pl.when(crossing)
     def _():
         for j in range(plane):
-            cross(j).start()
-
-    relay(0).start()
-    for j in range(1, plane):
-        gather(j).wait_recv()
-        relay(j).start()
+            pltpu.make_async_remote_copy(
+                place(cells, k), place((1 + pair) * cells, k), gs.at[1], gr.at[1],
+                device_id=(flat(j), far), device_id_type=MESH).start()
+
+    ones = jnp.ones((16, phases), jnp.bfloat16)
+    nrm[...] = jnp.zeros_like(nrm)
 
     @pl.loop(0, KSIDE)
     def _(b):
+        total = None
+        for a in range(KSIDE):
+            term = jnp.dot(ones, kbuf[b, a], preferred_element_type=jnp.float32)
+            total = term if total is None else total + term
+        nrm[...] += total
+
+    relay = pltpu.make_async_remote_copy(
+        rx.at[:, pl.ds(cells, cells), :], rx.at[:, pl.ds(pl.multiple_of((1 - pair) * cells, cells), cells), :],
+        gs.at[2], gr.at[2], device_id=(d, t + pair), device_id_type=MESH)
+    landed(precv.at[others], gr.at[0])
+    relay.start()
+
+    @pl.loop(0, KSIDE, unroll=3)
+    def _(b):
         parts[b] = partial_sums(rx, kbuf.at[b], -1, cells, True, False)
 
-    for j in range(plane):
-        relay(j).wait_recv()
-
-    @pl.when(crossing)
-    def _():
-        for j in range(plane):
-            cross(j).wait_recv()
+    relay.wait_recv()
+
+    @pl.when(crossing)
+    def _():
+        landed(rx.at[:, pl.ds(0, cells), :], gr.at[1])
 
     for b in range(KSIDE):
         total = parts[b] + partial_sums(rx, kbuf.at[b], -1, cells, False, False)
@@ -273,17 +261,14 @@
         scaled = acc[f * cells:(f + 1) * cells, :] / norm
         out[f, :, 0, :] = vbuf[f, :, 0, :] * scaled.T
 
-    for copy in sends:
-        copy.wait_send()
-    for j in range(1, plane):
-        gather(j).wait_send()
-    for j in range(plane):
-        relay(j).wait_send()
-
-    @pl.when(crossing)
-    def _():
-        for j in range(plane):
-            cross(j).wait_send()
+    landed(precv.at[others], ps)
+    landed(zrecv.at[pl.ds(1, lines - 1)], zs)
+    landed(precv.at[others], gs.at[0])
+    relay.wait_send()
+
+    @pl.when(crossing)
+    def _():
+        landed(rx.at[:, pl.ds(0, cells), :], gs.at[1])
 
     @pl.when(t < tiles - 1)
     def _():
@@ -319,19 +304,18 @@
             pltpu.VMEM((rows, phases), f32),
             pltpu.VMEM((rows, phases), f32),
             pltpu.VMEM((KSIDE, rows, phases), f32),
-            pltpu.VMEM((8, phases), f32),
+            pltpu.VMEM((16, phases), f32),
             pltpu.VMEM((rows, phases), bf16),
             pltpu.VMEM((plane, block, phases), bf16),
             pltpu.VMEM((block, phases), bf16),
             pltpu.VMEM((lines, block, phases), bf16),
             dma((KSIDE,)), dma((2,)), dma((2,)), dma((2,)),
-            dma((plane,)), dma((plane,)), dma((lines,)), dma((lines,)),
-            dma((3, plane)), dma((3, plane)),
+            dma, dma, dma, dma, dma((3,)), dma((3,)),
             pltpu.SemaphoreType.REGULAR((4,)),
         ],
         compiler_params=pltpu.CompilerParams(
-            collective_id=0, has_side_effects=True),
-    )(vol, ker, meas)
+            collective_id=0, has_side_effects=True, vmem_limit_bytes=48 << 20),
+    )(*(pltpu.with_memory_space_constraint(x, pltpu.HBM) for x in (vol, ker, meas)))
     return out.transpose(0, 2, 1, 3)
 
 

time: 40.6 us -> 38.2 us (0.941)
  Pallas kernels: 38.8 us -> 37.4 us
  local copies, waits for them, and re-layouts: 1.64 us -> 0.69 us
    pallas_call x1, Pallas kernels: 38.8 us -> 37.4 us  [local(): pl.pallas_call(functools.partial(step, plane, lines, tiles), out_shape=ja...]
    unnamed x1, local copies, waits for them, and re-layouts: 1.64 us -> 0.69 us
where the time goes in v3:
time: 38.2 us; the launch traced here: 38.1 us
  Pallas kernels  37.4 us (98%)
  local copies, waits for them, and re-layouts  0.69 us (2%)
    pallas_call x1, Pallas kernels, local(): pl.pallas_call(functools.partial(step, plane, lines, tiles), out_shape=ja...  37.4 us

profile of v3, /device:TPU:1, one launch (start us, length us, event | category | flops | bytes accessed | tf_op | source)
XLA Modules:
  0.0 38.1 jit_solution(6961894034138692915)
XLA Ops:
  0.0 37.4 %shard_map.37 = f32[2,225,1,128]{3,2,1,0:T(1,128)S(1)} custom-call(f32[2,225,1,128]{3,2,1,0:T(1,128)} %bitcast.8, bf16[9,9,225,225]{3,2,1,0:T(8,128)(2,1)} %bitcast.7, f32[225,2,128]{2,1,0:T(2,128)} %bitcast.9), custom_call_target="tpu_custom_call" | custom-call | tf_op jit(solution)/shard_map/pallas_call | solution.py:293
  37.5 0.7 %copy.5 = f32[2,1,225,128]{3,1,2,0:T(1,128)} copy(f32[2,1,225,128]{3,1,2,0:T(1,128)S(1)} %bitcast.6) | data formatting | bytes 460800

commit v4 on v3

--- a/solution.py
+++ b/solution.py
@@ -11,6 +11,7 @@
 HALF = 4
 COLS = 32
 FRAMES = 2
+AHEAD = 4
 MESH = pl.DeviceIdType.MESH
 
 
@@ -104,10 +105,9 @@
         vx[:, 2 * cells:, :] = jnp.zeros((FRAMES, cells, phases), jnp.bfloat16)
         rx[:, 2 * cells:, :] = jnp.zeros((FRAMES, cells, phases), jnp.bfloat16)
 
+    for b in range(AHEAD):
+        load_kernel(b).start()
     load_vol.wait()
-    for b in range(KSIDE):
-        load_kernel(b).start()
-    load_meas.start()
     for f in range(FRAMES):
         vx[f, cells:2 * cells, :] = vbuf[f, :, 0, :].T.astype(jnp.bfloat16)
 
@@ -132,13 +132,16 @@
         tell(round_sem.at[1], along(2), t)
         tell(round_sem.at[2], across, t)
 
-    load_meas.wait()
-    for f in range(FRAMES):
-        mt[f * cells:(f + 1) * cells, :] = mbuf[:, f, :].T
+    load_meas.start()
 
     @pl.loop(0, KSIDE)
     def _(b):
         load_kernel(b).wait()
+
+        @pl.when(b < KSIDE - AHEAD)
+        def _():
+            load_kernel(b + AHEAD).start()
+
         parts[b] = partial_sums(vx, kbuf.at[b], 1, cells, True, True)
 
     if relayed:
@@ -187,6 +190,10 @@
         pltpu.make_async_copy(ref, ref, sem).wait()
 
     others = pl.ds(1, plane - 1)
+    load_meas.wait()
+    for f in range(FRAMES):
+        mt[f * cells:(f + 1) * cells, :] = mbuf[:, f, :].T
+
     mine = pl.ds(pl.multiple_of(k * block, block), block)
     part = acc[mine, :]
     landed(precv.at[others], pr)

time: 38.2 us -> 35.4 us (0.927)
  Pallas kernels: 37.4 us -> 34.6 us
    pallas_call x1, Pallas kernels: 37.4 us -> 34.6 us  [local(): pl.pallas_call(functools.partial(step, plane, lines, tiles), out_shape=ja...]
where the time goes in v4:
time: 35.4 us; the launch traced here: 35.3 us
  Pallas kernels  34.6 us (98%)
  local copies, waits for them, and re-layouts  0.69 us (2%)
    pallas_call x1, Pallas kernels, local(): pl.pallas_call(functools.partial(step, plane, lines, tiles), out_shape=ja...  34.6 us

profile of v4, /device:TPU:1, one launch (start us, length us, event | category | flops | bytes accessed | tf_op | source)
XLA Modules:
  0.0 35.3 jit_solution(18198558279486652626)
XLA Ops:
  0.0 34.6 %shard_map.37 = f32[2,225,1,128]{3,2,1,0:T(1,128)S(1)} custom-call(f32[2,225,1,128]{3,2,1,0:T(1,128)} %bitcast.8, bf16[9,9,225,225]{3,2,1,0:T(8,128)(2,1)} %bitcast.7, f32[225,2,128]{2,1,0:T(2,128)} %bitcast.9), custom_call_target="tpu_custom_call" | custom-call | tf_op jit(solution)/shard_map/pallas_call | solution.py:300
  34.6 0.7 %copy.5 = f32[2,1,225,128]{3,1,2,0:T(1,128)} copy(f32[2,1,225,128]{3,1,2,0:T(1,128)S(1)} %bitcast.6) | data formatting | bytes 460800

commit v5 on v4

--- a/solution.py
+++ b/solution.py
@@ -75,6 +75,9 @@
 
     across = z * plane + (k + plane // 2) % plane
     barrier = pltpu.get_barrier_semaphore()
+    tell(barrier, d, t + pair)
+    for b in range(AHEAD):
+        load_kernel(b).start()
     if relayed:
         row = z * plane + (k // 4) * 4
         for j in range(1, 4):
@@ -89,7 +92,6 @@
         for j in range(1, lines):
             tell(barrier, along(j), t)
         near = plane + lines - 2
-    tell(barrier, d, t + pair)
 
     @pl.when(crossing)
     def _():
@@ -105,8 +107,6 @@
         vx[:, 2 * cells:, :] = jnp.zeros((FRAMES, cells, phases), jnp.bfloat16)
         rx[:, 2 * cells:, :] = jnp.zeros((FRAMES, cells, phases), jnp.bfloat16)
 
-    for b in range(AHEAD):
-        load_kernel(b).start()
     load_vol.wait()
     for f in range(FRAMES):
         vx[f, cells:2 * cells, :] = vbuf[f, :, 0, :].T.astype(jnp.bfloat16)
@@ -201,7 +201,7 @@
         part += precv[j].astype(jnp.float32)
 
     zsend[...] = part.astype(jnp.bfloat16)
-    for j in range(1, lines):
+    for j in sorted(range(1, lines), key=lambda j: -min(j, lines - j)):
         pltpu.make_async_remote_copy(
             zsend, zrecv.at[j], zs, zr, device_id=(along(j), t), device_id_type=MESH).start()
     landed(zrecv.at[pl.ds(1, lines - 1)], zr)
@@ -219,17 +219,17 @@
 
     rx[fk, pl.ds(pl.multiple_of(cells + rk, block), block), :] = ratio
 
+    @pl.when(crossing)
+    def _():
+        for j in range(plane):
+            pltpu.make_async_remote_copy(
+                place(cells, k), place((1 + pair) * cells, k), gs.at[1], gr.at[1],
+                device_id=(flat(j), far), device_id_type=MESH).start()
+
     for j in range(1, plane):
         pltpu.make_async_remote_copy(
             place(cells, k), place(cells, k), gs.at[0], gr.at[0],
             device_id=(flat(j), t), device_id_type=MESH).start()
-
-    @pl.when(crossing)
-    def _():
-        for j in range(plane):
-            pltpu.make_async_remote_copy(
-                place(cells, k), place((1 + pair) * cells, k), gs.at[1], gr.at[1],
-                device_id=(flat(j), far), device_id_type=MESH).start()
 
     ones = jnp.ones((16, phases), jnp.bfloat16)
     nrm[...] = jnp.zeros_like(nrm)

time: 35.4 us -> 35.2 us (level)
  no operation moved by 1% of the time
where the time goes in v5:
time: 35.2 us; the launch traced here: 35.1 us
  Pallas kernels  34.4 us (98%)
  local copies, waits for them, and re-layouts  0.69 us (2%)
    pallas_call x1, Pallas kernels, local(): pl.pallas_call(functools.partial(step, plane, lines, tiles), out_shape=ja...  34.4 us

profile of v5, /device:TPU:1, one launch (start us, length us, event | category | flops | bytes accessed | tf_op | source)
XLA Modules:
  0.0 35.1 jit_solution(4737908485678535649)
XLA Ops:
  0.0 34.4 %shard_map.37 = f32[2,225,1,128]{3,2,1,0:T(1,128)S(1)} custom-call(f32[2,225,1,128]{3,2,1,0:T(1,128)} %bitcast.8, bf16[9,9,225,225]{3,2,1,0:T(8,128)(2,1)} %bitcast.7, f32[225,2,128]{2,1,0:T(2,128)} %bitcast.9), custom_call_target="tpu_custom_call" | custom-call | tf_op jit(solution)/shard_map/pallas_call | solution.py:300
  34.4 0.7 %copy.5 = f32[2,1,225,128]{3,1,2,0:T(1,128)} copy(f32[2,1,225,128]{3,1,2,0:T(1,128)S(1)} %bitcast.6) | data formatting | bytes 460800

commit v6 on v5

--- a/solution.py
+++ b/solution.py
@@ -180,7 +180,7 @@
         pl.semaphore_wait(round_sem.at[3], 1)
 
     psend[...] = acc[...].astype(jnp.bfloat16)
-    for j in range(1, plane):
+    for j in sorted(range(1, plane), key=lambda j: abs(2 - j % 4)):
         peer = (k + j) % plane
         pltpu.make_async_remote_copy(
             psend.at[pl.ds(pl.multiple_of(peer * block, block), block), :], precv.at[j], ps, pr,
@@ -221,12 +221,12 @@
 
     @pl.when(crossing)
     def _():
-        for j in range(plane):
+        for j in sorted(range(plane), key=lambda j: abs(2 - j % 4)):
             pltpu.make_async_remote_copy(
                 place(cells, k), place((1 + pair) * cells, k), gs.at[1], gr.at[1],
                 device_id=(flat(j), far), device_id_type=MESH).start()
 
-    for j in range(1, plane):
+    for j in sorted(range(1, plane), key=lambda j: abs(2 - j % 4)):
         pltpu.make_async_remote_copy(
             place(cells, k), place(cells, k), gs.at[0], gr.at[0],
             device_id=(flat(j), t), device_id_type=MESH).start()

time: 35.2 us -> 34.8 us (0.989)
  no operation moved by 1% of the time
where the time goes in v6:
time: 34.8 us
  Pallas kernels  34.1 us (98%)
  local copies, waits for them, and re-layouts  0.69 us (2%)
    pallas_call x1, Pallas kernels, local(): pl.pallas_call(functools.partial(step, plane, lines, tiles), out_shape=ja...  34.1 us

profile of v6, /device:TPU:1, one launch (start us, length us, event | category | flops | bytes accessed | tf_op | source)
XLA Modules:
  0.0 34.8 jit_solution(18312857969987543271)
XLA Ops:
  0.0 34.1 %shard_map.37 = f32[2,225,1,128]{3,2,1,0:T(1,128)S(1)} custom-call(f32[2,225,1,128]{3,2,1,0:T(1,128)} %bitcast.8, bf16[9,9,225,225]{3,2,1,0:T(8,128)(2,1)} %bitcast.7, f32[225,2,128]{2,1,0:T(2,128)} %bitcast.9), custom_call_target="tpu_custom_call" | custom-call | tf_op jit(solution)/shard_map/pallas_call | solution.py:300
  34.1 0.7 %copy.5 = f32[2,1,225,128]{3,1,2,0:T(1,128)} copy(f32[2,1,225,128]{3,1,2,0:T(1,128)S(1)} %bitcast.6) | data formatting | bytes 460800
